TPU v7x, 128 devices: a whole 4x4x4 slice. The times are simulated.
128 devices in a mesh: sector: 8 (over z, core), mode: 16 (over y, x).
Axes of the slice: x: 4, y: 4, z: 4, core: 2. Of those that a mesh axis runs over, the one named last changes fastest.
Arguments:
- modes: bfloat16 [256, 3, 32, 80, 128], P('mode', None, 'sector'), may hold values from -0.1875 to 0.1875
- thickness: float32 [32, 80, 128], P('sector'), may hold values from -6 to 6
- stiff_taps: float32 [27], replicated, may hold values from -1.25 to 1.25
- mass_taps: float32 [27], replicated, may hold values from 0.02 to 0.2
- eigenvalues: float32 [256], P('mode'), may hold values from 0.5 to 2
Outputs:
- sensitivity: float32 [256, 256], P('sector', 'mode')
All inputs are finite; a program needn't handle non-finite values.
Results may differ from a plain program's by a relative error of at most 0.0029.
Values may be sent and summed in bfloat16 or wider, within the bound.
A program may use at most 64 MiB of HBM per device.

v0:
```python
import jax
import jax.numpy as jnp
from jax import lax
from jax.sharding import PartitionSpec as P


def extended(cells, sides, width):
    for axis, dim in sides:
        count = lax.axis_size(axis)
        ends = count - 1
        head = lax.slice_in_dim(cells, 0, width, axis=dim)
        tail = lax.slice_in_dim(cells, cells.shape[dim] - width, cells.shape[dim], axis=dim)
        cells = jnp.concatenate(
            [
                lax.ppermute(tail, axis, [(i, (i + 1) % count) for i in range(ends)]),
                cells,
                lax.ppermute(head, axis, [((i + 1) % count, i) for i in range(ends)]),
            ],
            axis=dim,
        )
    return cells


def stencil(field, padded_thick, stiff_taps, mass_taps, lams):
    size_x = field.shape[2] - 2
    size_y = field.shape[3] - 2
    size_z = field.shape[4] - 2
    shape_out = (field.shape[0], field.shape[1], size_x, size_y, size_z)
    centre = padded_thick[1 : 1 + size_x, 1 : 1 + size_y, 1 : 1 + size_z]
    stiff_acc = jnp.zeros(shape_out, jnp.float32)
    mass_acc = jnp.zeros(shape_out, jnp.float32)
    for aoff in range(3):
        for boff in range(3):
            for doff in range(3):
                index = 9 * aoff + 3 * boff + doff
                coeff = 0.5 * (
                    centre
                    + padded_thick[aoff : aoff + size_x, boff : boff + size_y, doff : doff + size_z]
                )
                moved = (
                    coeff
                    * field[:, :, aoff : aoff + size_x, boff : boff + size_y, doff : doff + size_z]
                )
                stiff_acc = stiff_acc + stiff_taps[index] * moved
                mass_acc = mass_acc + mass_taps[index] * moved
    return (stiff_acc - lams[:, None, None, None, None] * mass_acc).astype(jnp.bfloat16)


def spread(whole):
    sectors = lax.axis_size("sector")
    groups = lax.axis_size("mode")
    total = whole.shape[0]
    arranged = whole.reshape(sectors, total // sectors, groups, total // groups)
    arranged = arranged.transpose(0, 2, 1, 3).reshape(
        sectors * groups * (total // sectors), total // groups
    )
    return lax.psum_scatter(arranged, ("sector", "mode"), scatter_dimension=0, tiled=True)


def on_device(modes, thickness, stiff_taps, mass_taps, eigenvalues):
    local_modes = modes.shape[0]
    size_z = modes.shape[4]
    thick_rim = extended(thickness, (("sector", 0),), 1)
    padded_thick = jnp.pad(thick_rim, ((0, 0), (1, 1), (1, 1)))
    planes = extended(modes, (("sector", 2),), 1)
    field = jnp.pad(planes.astype(jnp.float32), ((0, 0), (0, 0), (0, 0), (1, 1), (1, 1)))
    loaded = stencil(field, padded_thick, stiff_taps, mass_taps, eigenvalues)
    flat_modes = modes.reshape(local_modes, -1, size_z)
    flat_loaded = loaded.reshape(local_modes, -1, size_z)
    all_modes, all_loaded = (
        lax.all_to_all(flat_modes, "mode", split_axis=1, concat_axis=0, tiled=True),
        lax.all_to_all(flat_loaded, "mode", split_axis=1, concat_axis=0, tiled=True),
    )
    whole = lax.dot_general(
        all_modes, all_loaded, (((1, 2), (1, 2)), ((), ())), preferred_element_type=jnp.float32
    )
    return spread(whole)


def solution(mesh):
    in_specs = (P("mode", None, "sector", None, None), P("sector", None, None), P(), P(), P("mode"))
    out_specs = P("sector", "mode")
    return jax.shard_map(
        on_device, mesh=mesh, in_specs=in_specs, out_specs=out_specs, check_vma=False
    )
```

profile of v0, /device:TPU:0, one launch (start us, length us, event | category | flops | bytes accessed | tf_op | source)
XLA Modules:
  0.0 861.1 jit_solution(12675278944696315850)
XLA Ops:
  6.5 0.8 fusion.56
  7.3 1.3 collective-permute-start
  8.6 1.3 collective-permute-start.1
  9.9 2.6 fusion.55
  12.6 5.3 collective-permute-start.2
  17.9 0.0 copy-start.3
  17.9 0.0 copy-start.4
  17.9 1.4 collective-permute-start.3
  19.4 6.5 copy.14
  25.9 7.1 all-to-all-start.1
  33.0 0.0 copy-start
  33.0 0.7 fusion.57
  33.7 0.7 fusion.58
  34.4 0.7 fusion.59
  35.2 0.7 fusion.60
  35.9 0.2 select_maximum_fusion
  36.1 0.2 fusion.53
  36.3 0.6 fusion.54
  37.0 0.9 maximum_convert_fusion
  38.0 96.1 %subtract_convert_fusion = bf16[16,3,4,80,128]{4,3,2,1,0:T(8,128)(2,1)S(1)} fusion(f32[16,3,6,80,128]{4,3,2,1,0:T(8,128)S(1)} %maximum_convert_fusion, f32[]{:T(128)} %bitcast.53, f32[]{:T(128)} %bitcast.52, f32[]{:T(128)} %bitcast.51, f32[]{:T(128)} %bitcast.50, f32[]{:T(128)} %bitcast.49, f32[]{:T(128)} %bitcast.48, f32[]{:T(128)} %bitcast.47, ...), kind=kLoop, calls=%fused_computation.51 | loop fusion | flops 267386880 | bytes 43746008 | tf_op jit(solution)/shard_map/convert_element_type | solution.py:46
  134.0 4.5 copy.12
  138.5 7.2 all-to-all-start
  145.7 0.0 reduce-scatter.4.cloned.1.call-start
  145.8 5.2 copy.15
  151.0 56.3 %all-to-all-done = bf16[16,960,128]{2,0,1:T(8,128)(2,1)} async-done(((bf16[16,960,128]{2,0,1:T(8,128)(2,1)}), bf16[16,960,128]{2,0,1:T(8,128)(2,1)}, u32[]{:S(2)}, u32[]{:S(2)}) %all-to-all-start) | async-done | bytes 3932192 | tf_op jit(solution)/shard_map/all_to_all | solution.py:72
  207.2 3.4 copy.13
  210.6 1.2 convolution_bitcast_fusion
  211.9 0.3 reshape.42
  212.1 2.0 copy.19
  214.1 0.0 reduce-scatter.4.cloned.1.call-update
  214.2 638.7 %reduce-scatter.4.cloned.1.call-done = f32[32,16]{1,0:T(8,128)} async-done(((f32[4096,16]{1,0:T(8,128)}), f32[32,16]{1,0:T(8,128)}) %reduce-scatter.4.cloned.1.call-update) | async-done | bytes 2064
  852.9 1.4 copy.18
  (14 shorter events, 0.0 us)
Async XLA Ops:
  7.3 28.5 %collective-permute-start = (f32[1,80,128]{2,1,0:T(8,128)S(1)}, f32[1,80,128]{2,1,0:T(8,128)S(1)}, u32[]{:S(2)}, u32[]{:S(2)}) collective-permute-start(f32[1,80,128]{2,1,0:T(8,128)S(1)} %get-tuple-element.34), channel_id=1, source_target_pairs={{0,16},{16,32},{32,48},{48,64},{64,80},{80,96},{96,112},{1,17},{17... | collective-permute-start | bytes 122888 | tf_op jit(solution)/shard_map/ppermute | solution.py:15
  8.6 27.2 %collective-permute-start.1 = (f32[1,80,128]{2,1,0:T(8,128)S(1)}, f32[1,80,128]{2,1,0:T(8,128)S(1)}, u32[]{:S(2)}, u32[]{:S(2)}) collective-permute-start(f32[1,80,128]{2,1,0:T(8,128)S(1)} %get-tuple-element.35), channel_id=1, source_target_pairs={{16,0},{32,16},{48,32},{64,48},{80,64},{96,80},{112,96},{17,1},{33... | collective-permute-start | bytes 122888 | tf_op jit(solution)/shard_map/ppermute | solution.py:17
  12.6 24.4 %collective-permute-start.2 = (bf16[16,3,1,80,128]{4,3,2,1,0:T(8,128)(2,1)}, bf16[16,3,1,80,128]{4,3,2,1,0:T(8,128)(2,1)S(1)}, u32[]{:S(2)}, u32[]{:S(2)}) collective-permute-start(bf16[16,3,1,80,128]{4,3,2,1,0:T(8,128)(2,1)} %get-tuple-element.5), channel_id=1, source_target_pairs={{0,16},{16,32},{32,48},{48,64},{64,80},{80,96},{96,112},{1,17},{17... | collective-permute-start | bytes 2949128 | tf_op jit(solution)/shard_map/ppermute | solution.py:15
  17.9 15.1 %copy-start.3 = (f32[27]{0:T(128)S(1)}, f32[27]{0:T(128)}, u32[]{:S(2)}) copy-start(f32[27]{0:T(128)} %param.7) | copy-start | bytes 328
  17.9 16.5 %copy-start.4 = (f32[27]{0:T(128)S(1)}, f32[27]{0:T(128)}, u32[]{:S(2)}) copy-start(f32[27]{0:T(128)} %param.8) | copy-start | bytes 328
  17.9 17.9 %copy-start.2 = (f32[4,80,128]{2,1,0:T(8,128)S(1)}, f32[4,80,128]{2,1,0:T(8,128)}, u32[]{:S(2)}) copy-start(f32[4,80,128]{2,1,0:T(8,128)} %param.6) | copy-start | bytes 491524
  17.9 19.1 %collective-permute-start.3 = (bf16[16,3,1,80,128]{4,3,2,1,0:T(8,128)(2,1)S(1)}, bf16[16,3,1,80,128]{4,3,2,1,0:T(8,128)(2,1)S(1)}, u32[]{:S(2)}, u32[]{:S(2)}) collective-permute-start(bf16[16,3,1,80,128]{4,3,2,1,0:T(8,128)(2,1)S(1)} %get-tuple-element.6), channel_id=1, source_target_pairs={{16,0},{32,16},{48,32},{64,48},{80,64},{96,80},{112,96},{17,1},{33... | collective-permute-start | bytes 2949128 | tf_op jit(solution)/shard_map/ppermute | solution.py:17
  25.9 112.6 %all-to-all-start.1 = ((bf16[16,960,128]{2,0,1:T(8,128)(2,1)}), bf16[16,960,128]{2,0,1:T(8,128)(2,1)}, u32[]{:S(2)}, u32[]{:S(2)}) async-start(bf16[16,960,128]{2,0,1:T(8,128)(2,1)} %bitcast.75), calls=%async_computation.1 | async-start | bytes 7864320 | tf_op jit(solution)/shard_map/all_to_all | solution.py:71
  33.0 4.0 copy-start
  37.0 1.0 copy-start.5
  138.5 68.7 %all-to-all-start = ((bf16[16,960,128]{2,0,1:T(8,128)(2,1)}), bf16[16,960,128]{2,0,1:T(8,128)(2,1)}, u32[]{:S(2)}, u32[]{:S(2)}) async-start(bf16[16,960,128]{2,0,1:T(8,128)(2,1)} %bitcast.76), calls=%async_computation | async-start | bytes 7864320 | tf_op jit(solution)/shard_map/all_to_all | solution.py:72
  145.7 707.1 %reduce-scatter.4.cloned.1.call-start = ((), (), s32[]{:S(2)}) async-start(), calls=%async_computation.3 | async-start | bytes 2113536
  207.2 3.4 copy-start.1
Sparse Core Ops, SparseCore 0:
  214.3 638.5 reduce-scatter.3
where the time goes:
time: 862 us; the launch traced here: 861 us
  waiting for transfers between devices  695 us (81%)
  other arithmetic  98.1 us (11%)
  local copies, waits for them, and re-layouts  29.5 us (3%)
  starting transfers between devices  23.6 us (3%)
  between operations  13.6 us (2%)
    unnamed x2, waiting for transfers between devices  639 us
    convert_element_type x1, other arithmetic, stencil(): (stiff_acc - lams[:, None, None, None, None] * mass_acc).astype(jnp.bfloa...  96.1 us
    all_to_all x1, waiting for transfers between devices, on_device(): lax.all_to_all(flat_loaded, 'mode', split_axis=1, concat_axis=0, tiled=True)  56.3 us
  transfers between devices with their start and end apart: 7, of which 2 were waited for; matrix products, arithmetic and copies ran while one was open for 14% of the time, Pallas kernels for 0%

commit v1 on v0

v1 whole, which is shorter than its diff:
```python
import functools

import jax
import jax.numpy as jnp
from jax import lax
from jax.experimental import pallas as pl
from jax.experimental.pallas import tpu as pltpu
from jax.sharding import PartitionSpec as P

MESH = pl.DeviceIdType.MESH
GROUPS = 16
SECTORS = 8
OWN = 15
ROWS = 16
PLANES = 4
NZ = 128
MODES = 256
NY = 80
ALL_ROWS = 240
PIECES = ((0, 0, 16), (1, 0, 16), (2, 0, 16), (3, 0, 4), (3, 4, 4), (3, 8, 4), (3, 12, 4))


def kernel(
    src, thick, stiff, mass, eig, out,
    m, images, thk, trow, tcol, taps, lamb, acc, sums, parts, blocks,
    send_sem, recv_sem, own_sem, rim_sem, thick_sem, lam_send, lam_recv, sum_send, sum_recv, blk_send, blk_recv,
):
    sec = lax.axis_index("sector")
    me = lax.axis_index("mode")
    me_x = lax.rem(me, 4)
    me_y = lax.div(me, 4)
    before = lax.rem(sec + SECTORS - 1, SECTORS)

    def peer(off):
        dx = lax.rem(off, 4)
        dy = lax.div(off, 4)
        return lax.rem(me_y + dy, 4) * 4 + lax.rem(me_x + dx, 4)

    def first_row(group):
        return jnp.minimum(group * OWN, ALL_ROWS - ROWS)

    m[:, :, ROWS] = jnp.zeros((PLANES + 1, GROUPS, 16, NZ), jnp.bfloat16)
    barrier = pltpu.get_barrier_semaphore()

    @pl.loop(1, GROUPS)
    def _(off):
        pl.semaphore_signal(barrier, inc=1, device_id=(sec, peer(off)), device_id_type=MESH)

    @pl.loop(1, SECTORS)
    def _(off):
        pl.semaphore_signal(
            barrier, inc=1, device_id=(lax.rem(sec + off, SECTORS), me), device_id_type=MESH
        )

    own_first = first_row(me)
    own = [
        pltpu.make_async_copy(
            src.at[plane, pl.ds(own_first, ROWS)], m.at[plane, me, pl.ds(0, ROWS)], own_sem.at[plane]
        )
        for plane in range(PLANES)
    ]
    for copy in own:
        copy.start()
    for j in range(GROUPS):
        lamb[me, j : j + 1, :] = jnp.full((1, NZ), eig[j], jnp.float32)
    pl.semaphore_wait(barrier, GROUPS - 1 + SECTORS - 1)

    def piece_copy(index, dest, origin):
        plane, row, rows = PIECES[index]
        return pltpu.make_async_remote_copy(
            src_ref=src.at[plane, pl.ds(first_row(dest) + row, rows)],
            dst_ref=m.at[plane, origin, pl.ds(row, rows)],
            send_sem=send_sem.at[index, dest],
            recv_sem=recv_sem.at[index, origin],
            device_id=(sec, dest),
            device_id_type=MESH,
        )

    def lam_copy(dest, origin):
        return pltpu.make_async_remote_copy(
            src_ref=lamb.at[me],
            dst_ref=lamb.at[origin],
            send_sem=lam_send.at[dest],
            recv_sem=lam_recv.at[origin],
            device_id=(sec, dest),
            device_id_type=MESH,
        )

    thick_copy = pltpu.make_async_remote_copy(
        src_ref=thick.at[0],
        dst_ref=thk,
        send_sem=thick_sem.at[0],
        recv_sem=thick_sem.at[1],
        device_id=(before, me),
        device_id_type=MESH,
    )
    thick_copy.start()
    for index in range(len(PIECES)):

        @pl.loop(1, GROUPS)
        def _(off, index=index):
            piece_copy(index, peer(off), me).start()

        if index == 0:

            @pl.loop(1, GROUPS)
            def _(off):
                lam_copy(peer(off), me).start()

    acc[...] = jnp.zeros_like(acc)
    tcol[:, ROWS] = jnp.zeros((PLANES + 1, NZ, NZ), jnp.float32)
    diff = lax.broadcasted_iota(jnp.int32, (NZ, NZ), 0) - lax.broadcasted_iota(
        jnp.int32, (NZ, NZ), 1
    )
    for ab in range(9):
        for half, table in enumerate((stiff, mass)):
            value = jnp.where(
                diff == 0,
                table[3 * ab + 1],
                jnp.where(
                    diff == 1,
                    table[3 * ab + 2],
                    jnp.where(diff == -1, table[3 * ab], 0.0),
                ),
            )
            taps[ab, :, half * NZ : (half + 1) * NZ] = 0.5 * value

    def thick_rows(plane, ref):
        @pl.loop(0, ROWS)
        def _(l):
            y = lax.rem(own_first + l, NY)
            trow[plane, pl.ds(l, 1), :] = ref[pl.ds(y, 1), :]

        column = jnp.transpose(trow[plane])
        for l in range(ROWS):
            tcol[plane, l] = jnp.broadcast_to(column[:, l : l + 1], (NZ, NZ))

    trow[...] = jnp.zeros_like(trow)
    for plane in range(PLANES):
        thick_rows(plane, thick.at[plane])
    thick_copy.wait()
    thick_rows(PLANES, thk)

    last_group = me == GROUPS - 1
    end_sector = sec == SECTORS - 1

    def source_row(l, b, cross_end):
        if b == 0:
            ok = jnp.where(last_group, l >= 1, l < ROWS - 1)
        else:
            low = l if b == 1 else l - 1
            ok = jnp.where(last_group, low >= 1, low >= 0) & (low < ROWS - 1)
            ok = ok & (lax.rem(own_first + low + 1, NY) != 0)
        if cross_end:
            ok = ok & jnp.logical_not(end_sector)
        return jnp.where(ok, l + b, ROWS)

    def image_of(l, plane_out, plane):
        centre = trow[plane_out, pl.ds(l, 1), :]
        fields, highs, lows = [], [], []
        for b in (-1, 0, 1):
            r = source_row(l, b, max(plane, plane_out) == PLANES)
            ab = 3 * (plane - plane_out + 1) + b + 1
            fields.append(m[plane, :, r].reshape(MODES, NZ))
            both = centre + tcol[plane, r]
            coeff = jnp.concatenate([both, both], axis=1) * taps[ab]
            high = coeff.astype(jnp.bfloat16)
            highs.append(high)
            lows.append((coeff - high.astype(jnp.float32)).astype(jnp.bfloat16))
        return jnp.dot(
            jnp.concatenate(fields + fields, axis=1),
            jnp.concatenate(highs + lows, axis=0),
            preferred_element_type=jnp.float32,
        )

    def row_step(l, plane, outs):
        loads, rows = [], []
        for plane_out, begun, complete in outs:
            image = image_of(l, plane_out, plane)
            if not begun:
                image = image + images[plane_out, l]
            if not complete:
                images[plane_out, l] = image
                continue
            lam = lamb[...].reshape(MODES, NZ)
            loads.append((image[:, :NZ] - lam * image[:, NZ:]).astype(jnp.bfloat16))
            rows.append(m[plane_out, :, l].reshape(MODES, NZ))
        if loads:
            gram = lax.dot_general(
                jnp.concatenate(loads, axis=1),
                jnp.concatenate(rows, axis=1),
                (((1,), (1,)), ((), ())),
                preferred_element_type=jnp.float32,
            )
            acc[...] += gram.reshape(GROUPS, 16, MODES)

    def process(plane, outs, low, high):
        @pl.loop(low, high)
        def _(l):
            row_step(l, plane, outs)

    def arrived(index):
        @pl.loop(1, GROUPS)
        def _(off):
            piece_copy(index, me, peer(off)).wait_recv()

    arrived(0)
    own[0].wait()
    rim = pltpu.make_async_remote_copy(
        src_ref=m.at[0],
        dst_ref=m.at[PLANES],
        send_sem=rim_sem.at[0],
        recv_sem=rim_sem.at[1],
        device_id=(before, me),
        device_id_type=MESH,
    )
    rim.start()

    @pl.loop(1, GROUPS)
    def _(off):
        lam_copy(me, peer(off)).wait_recv()

    process(0, [(0, True, False), (1, True, False)], 0, ROWS)
    arrived(1)
    own[1].wait()
    process(1, [(0, False, True), (1, False, False), (2, True, False)], 0, ROWS)
    arrived(2)
    own[2].wait()
    process(2, [(1, False, True), (2, False, False), (3, True, False)], 0, ROWS)
    rim.wait()
    process(4, [(3, False, False)], 0, ROWS)
    own[3].wait()
    for quarter in range(4):
        arrived(3 + quarter)
        process(
            3,
            [(2, False, True), (3, False, True), (4, True, True)],
            max(0, 4 * quarter - 1),
            ROWS if quarter == 3 else 4 * quarter + 3,
        )

    def sum_copy(dest, origin):
        return pltpu.make_async_remote_copy(
            src_ref=acc.at[dest],
            dst_ref=sums.at[origin],
            send_sem=sum_send.at[dest],
            recv_sem=sum_recv.at[origin],
            device_id=(sec, dest),
            device_id_type=MESH,
        )

    @pl.loop(1, GROUPS)
    def _(off):
        sum_copy(peer(off), me).start()

    sums[me] = acc[me]

    @pl.loop(1, GROUPS)
    def _(off):
        sum_copy(me, peer(off)).wait_recv()

    total = sums[0]
    for p in range(1, GROUPS):
        total = total + sums[p]
    for s in range(SECTORS):
        parts[s, :, 0:32] = total[:, 32 * s : 32 * s + 32]
        parts[s, :, 32:NZ] = jnp.zeros((16, NZ - 32), jnp.float32)

    def block_copy(dest, origin):
        return pltpu.make_async_remote_copy(
            src_ref=parts.at[dest],
            dst_ref=blocks.at[origin],
            send_sem=blk_send.at[dest],
            recv_sem=blk_recv.at[origin],
            device_id=(dest, me),
            device_id_type=MESH,
        )

    @pl.loop(1, SECTORS)
    def _(off):
        block_copy(lax.rem(sec + off, SECTORS), sec).start()

    blocks[sec] = parts[sec]

    @pl.loop(1, SECTORS)
    def _(off):
        block_copy(sec, lax.rem(sec + off, SECTORS)).wait_recv()

    block = blocks[0]
    for s in range(1, SECTORS):
        block = block + blocks[s]
    out[...] = jnp.transpose(block)[0:32, :]

    for index in range(len(PIECES)):

        @pl.loop(1, GROUPS)
        def _(off, index=index):
            piece_copy(index, peer(off), me).wait_send()

    @pl.loop(1, GROUPS)
    def _(off):
        lam_copy(peer(off), me).wait_send()
        sum_copy(peer(off), me).wait_send()

    @pl.loop(1, SECTORS)
    def _(off):
        block_copy(lax.rem(sec + off, SECTORS), sec).wait_send()


def on_device(modes, thickness, stiff_taps, mass_taps, eigenvalues):
    src = modes.transpose(2, 1, 3, 0, 4).reshape(PLANES, ALL_ROWS, 16, NZ)
    smem = pl.BlockSpec(memory_space=pltpu.SMEM)
    vmem = pl.BlockSpec(memory_space=pltpu.VMEM)
    dma = pltpu.SemaphoreType.DMA
    f32 = jnp.float32
    return pl.pallas_call(
        kernel,
        out_shape=jax.ShapeDtypeStruct((32, 16), f32),
        in_specs=[pl.BlockSpec(memory_space=pl.ANY), vmem, smem, smem, smem],
        out_specs=vmem,
        scratch_shapes=[
            pltpu.VMEM((PLANES + 1, GROUPS, ROWS + 1, 16, NZ), jnp.bfloat16),
            pltpu.VMEM((PLANES, ROWS, MODES, 2 * NZ), f32),
            pltpu.VMEM((NY, NZ), f32),
            pltpu.VMEM((PLANES + 1, NZ, NZ), f32),
            pltpu.VMEM((PLANES + 1, ROWS + 1, NZ, NZ), f32),
            pltpu.VMEM((9, NZ, 2 * NZ), f32),
            pltpu.VMEM((GROUPS, 16, NZ), f32),
            pltpu.VMEM((GROUPS, 16, MODES), f32),
            pltpu.VMEM((GROUPS, 16, MODES), f32),
            pltpu.VMEM((SECTORS, 16, NZ), f32),
            pltpu.VMEM((SECTORS, 16, NZ), f32),
            dma((len(PIECES), GROUPS)),
            dma((len(PIECES), GROUPS)),
            dma((PLANES,)),
            dma((2,)),
            dma((2,)),
            dma((GROUPS,)),
            dma((GROUPS,)),
            dma((GROUPS,)),
            dma((GROUPS,)),
            dma((SECTORS,)),
            dma((SECTORS,)),
        ],
        compiler_params=pltpu.CompilerParams(
            collective_id=0, has_side_effects=True, vmem_limit_bytes=48 * 2**20
        ),
    )(src, thickness, stiff_taps, mass_taps, eigenvalues)


def solution(mesh):
    in_specs = (P("mode", None, "sector", None, None), P("sector", None, None), P(), P(), P("mode"))
    return jax.shard_map(
        on_device, mesh=mesh, in_specs=in_specs, out_specs=P("sector", "mode"), check_vma=False
    )
```

time: 862 us -> 98.5 us (0.11)
  waiting for transfers between devices: 695 us -> 0 us
  other arithmetic: 98.1 us -> 0 us
  Pallas kernels: 0 us -> 91.9 us
  local copies, waits for them, and re-layouts: 29.5 us -> 5.37 us
  starting transfers between devices: 23.6 us -> 0 us
  between operations: 13.6 us -> 0.04 us
    unnamed x2 -> x0, waiting for transfers between devices: 639 us -> none
    convert_element_type x2 -> x0, other arithmetic: 97 us -> none  [the longest x1 96.1 us: stencil(): (stiff_acc - lams[:, None, None, None, None] * mass_acc).astype(jnp.bfloa...]
    pallas_call x0 -> x1, Pallas kernels: none -> 91.9 us  [on_device(): pl.pallas_call(kernel, out_shape=jax.ShapeDtypeStruct((32, 16), f32), in_...]
    all_to_all x2 -> x0, waiting for transfers between devices: 56.3 us -> none  [the longest x1 56.3 us: on_device(): lax.all_to_all(flat_loaded, 'mode', split_axis=1, concat_axis=0, tiled=True)]
    all_to_all x2 -> x0, starting transfers between devices: 14.3 us -> none  [the longest x1 7.2 us: on_device(): lax.all_to_all(flat_loaded, 'mode', split_axis=1, concat_axis=0, tiled=True)]
    unnamed x15 -> x8, local copies, waits for them, and re-layouts: 9.95 us -> 0.01 us
    ppermute x4 -> x0, starting transfers between devices: 9.31 us -> none  [the longest x2 6.59 us: extended(): lax.ppermute(tail, axis, [(i, (i + 1) % count) for i in range(ends)])]
  transfers between devices with their start and end apart: 7 -> 0, of which waited for: 2 -> 0; matrix products, arithmetic and copies ran while one was open for 14% -> 0% of each run, Pallas kernels for 0% -> 0%
where the time goes in v1:
time: 98.5 us; the launch traced here: 97.3 us
  Pallas kernels  91.9 us (93%)
  local copies, waits for them, and re-layouts  5.37 us (5%)
    pallas_call x1, Pallas kernels, on_device(): pl.pallas_call(kernel, out_shape=jax.ShapeDtypeStruct((32, 16), f32), in_...  91.9 us
    transpose x1, local copies, waits for them, and re-layouts, on_device(): src = modes.transpose(2, 1, 3, 0, 4).reshape(PLANES, ALL_ROWS, 16, NZ)  4.68 us

profile of v1, /device:TPU:0, one launch (start us, length us, event | category | flops | bytes accessed | tf_op | source)
XLA Modules:
  0.0 97.3 jit_solution(17827924966675474442)
XLA Ops:
  0.0 0.0 copy-start
  0.0 0.0 copy-start.1
  0.0 0.0 copy-start.2
  0.0 0.0 copy-start.3
  0.0 4.7 %copy.6 = bf16[4,3,80,16,128]{4,3,2,1,0:T(8,128)(2,1)S(1)} copy(bf16[4,3,80,16,128]{4,2,0,1,3:T(8,128)(2,1)} %bitcast.3) | data formatting | bytes 7864320 | tf_op jit(solution)/shard_map/transpose | solution.py:311
  4.7 0.0 copy-done
  4.7 0.0 copy-done.1
  4.7 0.0 copy-done.2
  4.7 0.0 copy-done.3
  4.7 91.9 %shard_map.55 = f32[32,16]{1,0:T(8,128)S(1)} custom-call(bf16[4,240,16,128]{3,2,1,0:T(8,128)(2,1)S(1)} %bitcast.2, f32[4,80,128]{2,1,0:T(8,128)S(1)} %copy-done, f32[27]{0:T(128)S(1)} %copy-done.1, f32[27]{0:T(128)S(1)} %copy-done.2, f32[16]{0:T(128)S(1)} %copy-done.3), custom_call_target="tpu_custom_call" | custom-call | tf_op jit(solution)/shard_map/pallas_call | solution.py:316
  96.7 0.7 copy.7
Async XLA Ops:
  0.0 4.7 %copy-start = (f32[4,80,128]{2,1,0:T(8,128)S(1)}, f32[4,80,128]{2,1,0:T(8,128)}, u32[]{:S(2)}) copy-start(f32[4,80,128]{2,1,0:T(8,128)} %thick.1) | copy-start | bytes 491524
  0.0 4.7 %copy-start.1 = (f32[27]{0:T(128)S(1)}, f32[27]{0:T(128)}, u32[]{:S(2)}) copy-start(f32[27]{0:T(128)} %stiff.1) | copy-start | bytes 328
  0.0 4.7 %copy-start.2 = (f32[27]{0:T(128)S(1)}, f32[27]{0:T(128)}, u32[]{:S(2)}) copy-start(f32[27]{0:T(128)} %mass.1) | copy-start | bytes 328
  0.0 4.7 %copy-start.3 = (f32[16]{0:T(128)S(1)}, f32[16]{0:T(128)}, u32[]{:S(2)}) copy-start(f32[16]{0:T(128)} %eig.1) | copy-start | bytes 196

commit v2 on v1

--- a/solution.py
+++ b/solution.py
@@ -17,12 +17,12 @@
 MODES = 256
 NY = 80
 ALL_ROWS = 240
-PIECES = ((0, 0, 16), (1, 0, 16), (2, 0, 16), (3, 0, 4), (3, 4, 4), (3, 8, 4), (3, 12, 4))
+PIECES = ((0, 0, 16), (1, 0, 16), (2, 0, 16), (3, 0, 8), (3, 8, 4), (3, 12, 4))
 
 
 def kernel(
     src, thick, stiff, mass, eig, out,
-    m, images, thk, trow, tcol, taps, lamb, acc, sums, parts, blocks,
+    m, images, matrix, single, coeffs, bands, thk, trow, lamb, acc, sums, parts, blocks,
     send_sem, recv_sem, own_sem, rim_sem, thick_sem, lam_send, lam_recv, sum_send, sum_recv, blk_send, blk_recv,
 ):
     sec = lax.axis_index("sector")
@@ -95,47 +95,86 @@
         device_id_type=MESH,
     )
     thick_copy.start()
-    for index in range(len(PIECES)):
-
+    def send(index):
         @pl.loop(1, GROUPS)
-        def _(off, index=index):
+        def _(off):
             piece_copy(index, peer(off), me).start()
 
-        if index == 0:
-
-            @pl.loop(1, GROUPS)
-            def _(off):
-                lam_copy(peer(off), me).start()
+    send(0)
+
+    @pl.loop(1, GROUPS)
+    def _(off):
+        lam_copy(peer(off), me).start()
+
+    for index in range(1, len(PIECES)):
+        send(index)
 
     acc[...] = jnp.zeros_like(acc)
-    tcol[:, ROWS] = jnp.zeros((PLANES + 1, NZ, NZ), jnp.float32)
-    diff = lax.broadcasted_iota(jnp.int32, (NZ, NZ), 0) - lax.broadcasted_iota(
-        jnp.int32, (NZ, NZ), 1
-    )
-    for ab in range(9):
-        for half, table in enumerate((stiff, mass)):
-            value = jnp.where(
-                diff == 0,
-                table[3 * ab + 1],
-                jnp.where(
-                    diff == 1,
-                    table[3 * ab + 2],
-                    jnp.where(diff == -1, table[3 * ab], 0.0),
-                ),
-            )
-            taps[ab, :, half * NZ : (half + 1) * NZ] = 0.5 * value
+    line = lax.broadcasted_iota(jnp.int32, (16, NZ), 0)
+    diff = line - lax.broadcasted_iota(jnp.int32, (16, NZ), 1)
+    for e in range(3):
+        bands[e] = jnp.where(lax.rem(diff + 1 - e + 128, 16) == 0, 1.0, 0.0).astype(jnp.bfloat16)
+    for i in range(8):
+        bands[3 + i] = jnp.where(jnp.abs(diff + 16 * i) <= 1, 1.0, 0.0).astype(jnp.bfloat16)
+    trow[...] = jnp.zeros_like(trow)
 
     def thick_rows(plane, ref):
         @pl.loop(0, ROWS)
         def _(l):
             y = lax.rem(own_first + l, NY)
-            trow[plane, pl.ds(l, 1), :] = ref[pl.ds(y, 1), :]
-
-        column = jnp.transpose(trow[plane])
-        for l in range(ROWS):
-            tcol[plane, l] = jnp.broadcast_to(column[:, l : l + 1], (NZ, NZ))
-
-    trow[...] = jnp.zeros_like(trow)
+            trow[1, plane, pl.ds(8 + l, 1), :] = ref[pl.ds(y, 1), :]
+
+        trow[0, plane] = pltpu.roll(trow[1, plane], 1, axis=1)
+        trow[2, plane] = pltpu.roll(trow[1, plane], NZ - 1, axis=1)
+
+    def coefficients(u, plane, plane_out):
+        centre = trow[1, plane_out, pl.ds(8, ROWS), :]
+        for b in range(3):
+            for e in range(3):
+                both = 0.5 * (centre + trow[e, plane, pl.ds(7 + b, ROWS), :])
+                k = 9 * (plane - plane_out + 1) + 3 * b + e
+                for half, table in enumerate((stiff, mass)):
+                    coeffs[u, b, half, e] = both * table[k]
+
+    def banded(u, l, put):
+        on = [bands[e] > 0 for e in range(2)]
+        tiles = {}
+        for b in range(3):
+            for half in range(2):
+                lines = [
+                    jnp.broadcast_to(coeffs[u, b, half, e, pl.ds(l, 1), :], (16, NZ)).astype(
+                        jnp.bfloat16
+                    )
+                    for e in range(3)
+                ]
+                tiles[b, half] = jnp.where(
+                    on[0], lines[0], jnp.where(on[1], lines[1], lines[2])
+                )
+        zero = jnp.zeros((16, NZ), jnp.bfloat16)
+        for i in range(8):
+            keep = bands[3 + i] > 0
+            for (b, half), tile in tiles.items():
+                first = b * NZ + 16 * i
+                put(
+                    slice(first, first + 16),
+                    slice(half * NZ, (half + 1) * NZ),
+                    jnp.where(keep, tile, zero),
+                )
+
+    def matrices(buf, pairs):
+        for u, (plane, plane_out) in enumerate(pairs):
+            coefficients(u, plane, plane_out)
+
+        @pl.loop(0, ROWS)
+        def _(l):
+
+            @pl.loop(0, len(pairs))
+            def _(u):
+                def put(rows, columns, tile):
+                    matrix[buf, u, l, rows, columns] = tile
+
+                banded(u, l, put)
+
     for plane in range(PLANES):
         thick_rows(plane, thick.at[plane])
     thick_copy.wait()
@@ -155,36 +194,32 @@
             ok = ok & jnp.logical_not(end_sector)
         return jnp.where(ok, l + b, ROWS)
 
-    def image_of(l, plane_out, plane):
-        centre = trow[plane_out, pl.ds(l, 1), :]
-        fields, highs, lows = [], [], []
+    def image_of(l, plane, plane_out, held):
+        fields = []
         for b in (-1, 0, 1):
             r = source_row(l, b, max(plane, plane_out) == PLANES)
-            ab = 3 * (plane - plane_out + 1) + b + 1
             fields.append(m[plane, :, r].reshape(MODES, NZ))
-            both = centre + tcol[plane, r]
-            coeff = jnp.concatenate([both, both], axis=1) * taps[ab]
-            high = coeff.astype(jnp.bfloat16)
-            highs.append(high)
-            lows.append((coeff - high.astype(jnp.float32)).astype(jnp.bfloat16))
         return jnp.dot(
-            jnp.concatenate(fields + fields, axis=1),
-            jnp.concatenate(highs + lows, axis=0),
+            jnp.concatenate(fields, axis=1),
+            held[...],
             preferred_element_type=jnp.float32,
         )
 
     def row_step(l, plane, outs):
         loads, rows = [], []
-        for plane_out, begun, complete in outs:
-            image = image_of(l, plane_out, plane)
+        for plane_out, buf, u, begun, complete in outs:
+            image = image_of(l, plane, plane_out, matrix.at[buf, u, l])
+            slot = plane_out % 3
             if not begun:
-                image = image + images[plane_out, l]
+                image = image + images[slot, l]
             if not complete:
-                images[plane_out, l] = image
+                images[slot, l] = image
                 continue
             lam = lamb[...].reshape(MODES, NZ)
-            loads.append((image[:, :NZ] - lam * image[:, NZ:]).astype(jnp.bfloat16))
-            rows.append(m[plane_out, :, l].reshape(MODES, NZ))
+            load = image[:, :NZ] - lam * image[:, NZ:]
+            high = load.astype(jnp.bfloat16)
+            loads += [high, (load - high.astype(jnp.float32)).astype(jnp.bfloat16)]
+            rows += [m[plane_out, :, l].reshape(MODES, NZ)] * 2
         if loads:
             gram = lax.dot_general(
                 jnp.concatenate(loads, axis=1),
@@ -204,6 +239,8 @@
         def _(off):
             piece_copy(index, me, peer(off)).wait_recv()
 
+    matrices(0, ((0, 0), (0, 1)))
+    matrices(1, ((1, 0), (1, 1), (1, 2)))
     arrived(0)
     own[0].wait()
     rim = pltpu.make_async_remote_copy(
@@ -220,23 +257,38 @@
     def _(off):
         lam_copy(me, peer(off)).wait_recv()
 
-    process(0, [(0, True, False), (1, True, False)], 0, ROWS)
+    process(0, [(0, 0, 0, True, False), (1, 0, 1, True, False)], 0, ROWS)
+    matrices(0, ((2, 1), (2, 2), (2, 3)))
     arrived(1)
     own[1].wait()
-    process(1, [(0, False, True), (1, False, False), (2, True, False)], 0, ROWS)
+    process(
+        1, [(0, 1, 0, False, True), (1, 1, 1, False, False), (2, 1, 2, True, False)], 0, ROWS
+    )
+    matrices(1, ((3, 2), (3, 3), (3, 4)))
+    rim.wait()
+    coefficients(0, PLANES, PLANES - 1)
+
+    @pl.loop(0, ROWS)
+    def _(l):
+        def put(rows, columns, tile):
+            single[rows, columns] = tile
+
+        banded(0, l, put)
+        images[(PLANES - 1) % 3, l] = image_of(l, PLANES, PLANES - 1, single)
+
     arrived(2)
     own[2].wait()
-    process(2, [(1, False, True), (2, False, False), (3, True, False)], 0, ROWS)
-    rim.wait()
-    process(4, [(3, False, False)], 0, ROWS)
+    process(
+        2, [(1, 0, 0, False, True), (2, 0, 1, False, False), (3, 0, 2, False, False)], 0, ROWS
+    )
     own[3].wait()
-    for quarter in range(4):
-        arrived(3 + quarter)
+    for index, low, high in ((3, 0, 7), (4, 7, 11), (5, 11, ROWS)):
+        arrived(index)
         process(
             3,
-            [(2, False, True), (3, False, True), (4, True, True)],
-            max(0, 4 * quarter - 1),
-            ROWS if quarter == 3 else 4 * quarter + 3,
+            [(2, 1, 0, False, True), (3, 1, 1, False, True), (4, 1, 2, True, True)],
+            low,
+            high,
         )
 
     def sum_copy(dest, origin):
@@ -320,11 +372,13 @@
         out_specs=vmem,
         scratch_shapes=[
             pltpu.VMEM((PLANES + 1, GROUPS, ROWS + 1, 16, NZ), jnp.bfloat16),
-            pltpu.VMEM((PLANES, ROWS, MODES, 2 * NZ), f32),
+            pltpu.VMEM((3, ROWS, MODES, 2 * NZ), f32),
+            pltpu.VMEM((2, 3, ROWS, 3 * NZ, 2 * NZ), jnp.bfloat16),
+            pltpu.VMEM((3 * NZ, 2 * NZ), jnp.bfloat16),
+            pltpu.VMEM((3, 3, 2, 3, ROWS, NZ), f32),
+            pltpu.VMEM((11, 16, NZ), jnp.bfloat16),
             pltpu.VMEM((NY, NZ), f32),
-            pltpu.VMEM((PLANES + 1, NZ, NZ), f32),
-            pltpu.VMEM((PLANES + 1, ROWS + 1, NZ, NZ), f32),
-            pltpu.VMEM((9, NZ, 2 * NZ), f32),
+            pltpu.VMEM((3, PLANES + 1, 32, NZ), f32),
             pltpu.VMEM((GROUPS, 16, NZ), f32),
             pltpu.VMEM((GROUPS, 16, MODES), f32),
             pltpu.VMEM((GROUPS, 16, MODES), f32),
@@ -343,7 +397,7 @@
             dma((SECTORS,)),
         ],
         compiler_params=pltpu.CompilerParams(
-            collective_id=0, has_side_effects=True, vmem_limit_bytes=48 * 2**20
+            collective_id=0, has_side_effects=True, vmem_limit_bytes=42 * 2**20
         ),
     )(src, thickness, stiff_taps, mass_taps, eigenvalues)
 

time: 98.5 us -> 87.9 us (0.89)
  Pallas kernels: 91.9 us -> 81.5 us
    pallas_call x1, Pallas kernels: 91.9 us -> 81.5 us  [on_device(): pl.pallas_call(kernel, out_shape=jax.ShapeDtypeStruct((32, 16), f32), in_...]
where the time goes in v2:
time: 87.9 us; the launch traced here: 86.9 us
  Pallas kernels  81.5 us (93%)
  local copies, waits for them, and re-layouts  5.37 us (6%)
    pallas_call x1, Pallas kernels, on_device(): pl.pallas_call(kernel, out_shape=jax.ShapeDtypeStruct((32, 16), f32), in_...  81.5 us
    transpose x1, local copies, waits for them, and re-layouts, on_device(): src = modes.transpose(2, 1, 3, 0, 4).reshape(PLANES, ALL_ROWS, 16, NZ)  4.68 us

profile of v2, /device:TPU:0, one launch (start us, length us, event | category | flops | bytes accessed | tf_op | source)
XLA Modules:
  0.0 86.9 jit_solution(9094648018396799178)
XLA Ops:
  0.0 0.0 copy-start
  0.0 0.0 copy-start.1
  0.0 0.0 copy-start.2
  0.0 0.0 copy-start.3
  0.0 4.7 %copy.6 = bf16[4,3,80,16,128]{4,3,2,1,0:T(8,128)(2,1)S(1)} copy(bf16[4,3,80,16,128]{4,2,0,1,3:T(8,128)(2,1)} %bitcast.3) | data formatting | bytes 7864320 | tf_op jit(solution)/shard_map/transpose | solution.py:363
  4.7 0.0 copy-done
  4.7 0.0 copy-done.1
  4.7 0.0 copy-done.2
  4.7 0.0 copy-done.3
  4.7 81.5 %shard_map.55 = f32[32,16]{1,0:T(8,128)S(1)} custom-call(bf16[4,240,16,128]{3,2,1,0:T(8,128)(2,1)S(1)} %bitcast.2, f32[4,80,128]{2,1,0:T(8,128)S(1)} %copy-done, f32[27]{0:T(128)S(1)} %copy-done.1, f32[27]{0:T(128)S(1)} %copy-done.2, f32[16]{0:T(128)S(1)} %copy-done.3), custom_call_target="tpu_custom_call" | custom-call | tf_op jit(solution)/shard_map/pallas_call | solution.py:368
  86.2 0.7 copy.7
Async XLA Ops:
  0.0 4.7 %copy-start = (f32[4,80,128]{2,1,0:T(8,128)S(1)}, f32[4,80,128]{2,1,0:T(8,128)}, u32[]{:S(2)}) copy-start(f32[4,80,128]{2,1,0:T(8,128)} %thick.1) | copy-start | bytes 491524
  0.0 4.7 %copy-start.1 = (f32[27]{0:T(128)S(1)}, f32[27]{0:T(128)}, u32[]{:S(2)}) copy-start(f32[27]{0:T(128)} %stiff.1) | copy-start | bytes 328
  0.0 4.7 %copy-start.2 = (f32[27]{0:T(128)S(1)}, f32[27]{0:T(128)}, u32[]{:S(2)}) copy-start(f32[27]{0:T(128)} %mass.1) | copy-start | bytes 328
  0.0 4.7 %copy-start.3 = (f32[16]{0:T(128)S(1)}, f32[16]{0:T(128)}, u32[]{:S(2)}) copy-start(f32[16]{0:T(128)} %eig.1) | copy-start | bytes 196

commit v3 on v2

--- a/solution.py
+++ b/solution.py
@@ -16,8 +16,9 @@
 NZ = 128
 MODES = 256
 NY = 80
+STEP = 4
 ALL_ROWS = 240
-PIECES = ((0, 0, 16), (1, 0, 16), (2, 0, 16), (3, 0, 8), (3, 8, 4), (3, 12, 4))
+PIECES = ((0, 0, 16), (1, 0, 16), (2, 0, 16), (3, 0, 16))
 
 
 def kernel(
@@ -205,8 +206,7 @@
             preferred_element_type=jnp.float32,
         )
 
-    def row_step(l, plane, outs):
-        loads, rows = [], []
+    def row_step(l, plane, outs, loads, rows):
         for plane_out, buf, u, begun, complete in outs:
             image = image_of(l, plane, plane_out, matrix.at[buf, u, l])
             slot = plane_out % 3
@@ -220,19 +220,21 @@
             high = load.astype(jnp.bfloat16)
             loads += [high, (load - high.astype(jnp.float32)).astype(jnp.bfloat16)]
             rows += [m[plane_out, :, l].reshape(MODES, NZ)] * 2
-        if loads:
-            gram = lax.dot_general(
-                jnp.concatenate(loads, axis=1),
-                jnp.concatenate(rows, axis=1),
-                (((1,), (1,)), ((), ())),
-                preferred_element_type=jnp.float32,
-            )
-            acc[...] += gram.reshape(GROUPS, 16, MODES)
 
     def process(plane, outs, low, high):
-        @pl.loop(low, high)
-        def _(l):
-            row_step(l, plane, outs)
+        @pl.loop(0, (high - low) // STEP)
+        def _(pair):
+            loads, rows = [], []
+            for other in range(STEP):
+                row_step(low + STEP * pair + other, plane, outs, loads, rows)
+            if loads:
+                gram = lax.dot_general(
+                    jnp.concatenate(loads, axis=1),
+                    jnp.concatenate(rows, axis=1),
+                    (((1,), (1,)), ((), ())),
+                    preferred_element_type=jnp.float32,
+                )
+                acc[...] += gram.reshape(GROUPS, 16, MODES)
 
     def arrived(index):
         @pl.loop(1, GROUPS)
@@ -282,7 +284,7 @@
         2, [(1, 0, 0, False, True), (2, 0, 1, False, False), (3, 0, 2, False, False)], 0, ROWS
     )
     own[3].wait()
-    for index, low, high in ((3, 0, 7), (4, 7, 11), (5, 11, ROWS)):
+    for index, low, high in ((3, 0, ROWS),):
         arrived(index)
         process(
             3,

time: 87.9 us -> 84.5 us (0.961)
  Pallas kernels: 81.5 us -> 77.9 us
    pallas_call x1, Pallas kernels: 81.5 us -> 77.9 us  [on_device(): pl.pallas_call(kernel, out_shape=jax.ShapeDtypeStruct((32, 16), f32), in_...]
where the time goes in v3:
time: 84.5 us; the launch traced here: 83.3 us
  Pallas kernels  77.9 us (92%)
  local copies, waits for them, and re-layouts  5.37 us (6%)
    pallas_call x1, Pallas kernels, on_device(): pl.pallas_call(kernel, out_shape=jax.ShapeDtypeStruct((32, 16), f32), in_...  77.9 us
    transpose x1, local copies, waits for them, and re-layouts, on_device(): src = modes.transpose(2, 1, 3, 0, 4).reshape(PLANES, ALL_ROWS, 16, NZ)  4.68 us

profile of v3, /device:TPU:0, one launch (start us, length us, event | category | flops | bytes accessed | tf_op | source)
XLA Modules:
  0.0 83.3 jit_solution(12866091401173916263)
XLA Ops:
  0.0 0.0 copy-start
  0.0 0.0 copy-start.1
  0.0 0.0 copy-start.2
  0.0 0.0 copy-start.3
  0.0 4.7 %copy.6 = bf16[4,3,80,16,128]{4,3,2,1,0:T(8,128)(2,1)S(1)} copy(bf16[4,3,80,16,128]{4,2,0,1,3:T(8,128)(2,1)} %bitcast.3) | data formatting | bytes 7864320 | tf_op jit(solution)/shard_map/transpose | solution.py:365
  4.7 0.0 copy-done
  4.7 0.0 copy-done.1
  4.7 0.0 copy-done.2
  4.7 0.0 copy-done.3
  4.7 77.9 %shard_map.55 = f32[32,16]{1,0:T(8,128)S(1)} custom-call(bf16[4,240,16,128]{3,2,1,0:T(8,128)(2,1)S(1)} %bitcast.2, f32[4,80,128]{2,1,0:T(8,128)S(1)} %copy-done, f32[27]{0:T(128)S(1)} %copy-done.1, f32[27]{0:T(128)S(1)} %copy-done.2, f32[16]{0:T(128)S(1)} %copy-done.3), custom_call_target="tpu_custom_call" | custom-call | tf_op jit(solution)/shard_map/pallas_call | solution.py:370
  82.7 0.7 copy.7
Async XLA Ops:
  0.0 4.7 %copy-start = (f32[4,80,128]{2,1,0:T(8,128)S(1)}, f32[4,80,128]{2,1,0:T(8,128)}, u32[]{:S(2)}) copy-start(f32[4,80,128]{2,1,0:T(8,128)} %thick.1) | copy-start | bytes 491524
  0.0 4.7 %copy-start.1 = (f32[27]{0:T(128)S(1)}, f32[27]{0:T(128)}, u32[]{:S(2)}) copy-start(f32[27]{0:T(128)} %stiff.1) | copy-start | bytes 328
  0.0 4.7 %copy-start.2 = (f32[27]{0:T(128)S(1)}, f32[27]{0:T(128)}, u32[]{:S(2)}) copy-start(f32[27]{0:T(128)} %mass.1) | copy-start | bytes 328
  0.0 4.7 %copy-start.3 = (f32[16]{0:T(128)S(1)}, f32[16]{0:T(128)}, u32[]{:S(2)}) copy-start(f32[16]{0:T(128)} %eig.1) | copy-start | bytes 196

commit v4 on v3

--- a/solution.py
+++ b/solution.py
@@ -18,7 +18,7 @@
 NY = 80
 STEP = 4
 ALL_ROWS = 240
-PIECES = ((0, 0, 16), (1, 0, 16), (2, 0, 16), (3, 0, 16))
+PIECES = ((0, 0, 16), (1, 0, 16), (2, 0, 16), (3, 0, 9), (3, 9, 7))
 
 
 def kernel(
@@ -284,7 +284,7 @@
         2, [(1, 0, 0, False, True), (2, 0, 1, False, False), (3, 0, 2, False, False)], 0, ROWS
     )
     own[3].wait()
-    for index, low, high in ((3, 0, ROWS),):
+    for index, low, high in ((3, 0, 8), (4, 8, ROWS)):
         arrived(index)
         process(
             3,

time: 84.5 us -> 81.8 us (0.968)
  Pallas kernels: 77.9 us -> 75.3 us
    pallas_call x1, Pallas kernels: 77.9 us -> 75.3 us  [on_device(): pl.pallas_call(kernel, out_shape=jax.ShapeDtypeStruct((32, 16), f32), in_...]
where the time goes in v4:
time: 81.8 us; the launch traced here: 80.7 us
  Pallas kernels  75.3 us (92%)
  local copies, waits for them, and re-layouts  5.37 us (7%)
    pallas_call x1, Pallas kernels, on_device(): pl.pallas_call(kernel, out_shape=jax.ShapeDtypeStruct((32, 16), f32), in_...  75.3 us
    transpose x1, local copies, waits for them, and re-layouts, on_device(): src = modes.transpose(2, 1, 3, 0, 4).reshape(PLANES, ALL_ROWS, 16, NZ)  4.68 us

profile of v4, /device:TPU:0, one launch (start us, length us, event | category | flops | bytes accessed | tf_op | source)
XLA Modules:
  0.0 80.7 jit_solution(6965295867234658853)
XLA Ops:
  0.0 0.0 copy-start
  0.0 0.0 copy-start.1
  0.0 0.0 copy-start.2
  0.0 0.0 copy-start.3
  0.0 4.7 %copy.6 = bf16[4,3,80,16,128]{4,3,2,1,0:T(8,128)(2,1)S(1)} copy(bf16[4,3,80,16,128]{4,2,0,1,3:T(8,128)(2,1)} %bitcast.3) | data formatting | bytes 7864320 | tf_op jit(solution)/shard_map/transpose | solution.py:365
  4.7 0.0 copy-done
  4.7 0.0 copy-done.1
  4.7 0.0 copy-done.2
  4.7 0.0 copy-done.3
  4.7 75.3 %shard_map.55 = f32[32,16]{1,0:T(8,128)S(1)} custom-call(bf16[4,240,16,128]{3,2,1,0:T(8,128)(2,1)S(1)} %bitcast.2, f32[4,80,128]{2,1,0:T(8,128)S(1)} %copy-done, f32[27]{0:T(128)S(1)} %copy-done.1, f32[27]{0:T(128)S(1)} %copy-done.2, f32[16]{0:T(128)S(1)} %copy-done.3), custom_call_target="tpu_custom_call" | custom-call | tf_op jit(solution)/shard_map/pallas_call | solution.py:370
  80.0 0.7 copy.7
Async XLA Ops:
  0.0 4.7 %copy-start = (f32[4,80,128]{2,1,0:T(8,128)S(1)}, f32[4,80,128]{2,1,0:T(8,128)}, u32[]{:S(2)}) copy-start(f32[4,80,128]{2,1,0:T(8,128)} %thick.1) | copy-start | bytes 491524
  0.0 4.7 %copy-start.1 = (f32[27]{0:T(128)S(1)}, f32[27]{0:T(128)}, u32[]{:S(2)}) copy-start(f32[27]{0:T(128)} %stiff.1) | copy-start | bytes 328
  0.0 4.7 %copy-start.2 = (f32[27]{0:T(128)S(1)}, f32[27]{0:T(128)}, u32[]{:S(2)}) copy-start(f32[27]{0:T(128)} %mass.1) | copy-start | bytes 328
  0.0 4.7 %copy-start.3 = (f32[16]{0:T(128)S(1)}, f32[16]{0:T(128)}, u32[]{:S(2)}) copy-start(f32[16]{0:T(128)} %eig.1) | copy-start | bytes 196
